TPU v7x, 32 devices: a whole 2x2x4 slice. The times are simulated.
32 devices in a mesh: grp: 8 (over z, y), blk: 4 (over x, core).
Axes of the slice: x: 2, y: 2, z: 4, core: 2. Of those that a mesh axis runs over, the one named last changes fastest.
Arguments:
- queries: bfloat16 [20480, 2048], P(('grp', 'blk')), may hold values from -6 to 6
- key_rows: bfloat16 [20480, 256], P(('grp', 'blk')), may hold values from -6 to 6
- value_rows: bfloat16 [20480, 256], P(('grp', 'blk')), may hold values from -6 to 6
- out_grad: bfloat16 [20480, 2048], P(('grp', 'blk')), may hold values from -12 to 12
- attn_out: bfloat16 [20480, 2048], P(('grp', 'blk')), may hold values from -6 to 6
- log_norm: float32 [20480, 16], P(('grp', 'blk')), may hold values from 4 to 7
- held_block: int32 [32], replicated, may hold values from 0 to 31, as said below
- key_block: int32 [32], replicated, may hold values from 0 to 31, as said below
Outputs:
- query_grad: bfloat16 [20480, 2048], P(('grp', 'blk'))
- key_grad: bfloat16 [20480, 256], P(('grp', 'blk'))
- value_grad: bfloat16 [20480, 256], P(('grp', 'blk'))
Inputs may be any that keep to these rules, and one draw needn't show every extreme that they name: held_block is a permutation of the 32 blocks. key_block[d] <= held_block[d] for every d; a key block may be paired with many query blocks or none.
All inputs are finite; a program needn't handle non-finite values.
Results may differ from a plain program's by a relative error of at most 0.0069.
Values may be sent and summed in bfloat16 or wider, within the bound.
A program may use at most 192 MiB of HBM per device.

v0:
```python
import jax
import jax.numpy as jnp
from jax import lax
from jax.sharding import PartitionSpec as P

H = 16
KVH = 2
DH = 128


def pair_grads(query, dout, outs, norms, kv_rows, diag):
    rows = query.shape[0]
    group = H // KVH
    scale = DH ** (-0.5)
    delta = jnp.sum(
        (dout.astype(jnp.float32) * outs.astype(jnp.float32)).reshape(rows, H, DH), axis=-1
    )
    row_ids = lax.broadcasted_iota(jnp.int32, (rows, rows), 0)
    col_ids = lax.broadcasted_iota(jnp.int32, (rows, rows), 1)
    keep = jnp.logical_or(jnp.logical_not(diag), col_ids <= row_ids)
    query_parts, key_parts, value_parts = ([], [], [])
    for head in range(KVH):
        width = group * DH
        q_head = query[:, head * width : (head + 1) * width].reshape(rows, group, DH)
        o_head = dout[:, head * width : (head + 1) * width].reshape(rows, group, DH)
        k_head = kv_rows[:, head * DH : (head + 1) * DH]
        v_head = kv_rows[:, (KVH + head) * DH : (KVH + head + 1) * DH]
        scores = (
            jnp.einsum("igd,jd->gij", q_head, k_head, preferred_element_type=jnp.float32) * scale
        )
        lse_head = jnp.transpose(norms[:, head * group : (head + 1) * group])[:, :, None]
        probs = jnp.where(keep[None], jnp.exp(scores - lse_head), 0.0)
        probs_low = probs.astype(jnp.bfloat16)
        dv_head = jnp.einsum("gij,igd->jd", probs_low, o_head, preferred_element_type=jnp.float32)
        dprob = jnp.einsum("igd,jd->gij", o_head, v_head, preferred_element_type=jnp.float32)
        delta_head = jnp.transpose(delta[:, head * group : (head + 1) * group])[:, :, None]
        dscore = (probs * (dprob - delta_head) * scale).astype(jnp.bfloat16)
        dq_head = jnp.einsum("gij,jd->igd", dscore, k_head, preferred_element_type=jnp.float32)
        dk_head = jnp.einsum("gij,igd->jd", dscore, q_head, preferred_element_type=jnp.float32)
        query_parts.append(dq_head.reshape(rows, width))
        key_parts.append(dk_head)
        value_parts.append(dv_head)
    query_grad = jnp.concatenate(query_parts, axis=1).astype(jnp.bfloat16)
    pair_term = jnp.concatenate(key_parts + value_parts, axis=1).astype(jnp.bfloat16)
    return (query_grad, pair_term)


def per_device(queries, key_rows, value_rows, out_grad, attn_out, log_norm, held_block, key_block):
    n_grp = lax.axis_size("grp")
    n_blk = lax.axis_size("blk")
    g_index = lax.axis_index("grp")
    b_index = lax.axis_index("blk")
    count = n_grp * n_blk
    own_index = g_index * n_blk + b_index
    positions = jnp.arange(count, dtype=jnp.int32)
    holder = jnp.sum(
        jnp.where(held_block[None, :] == key_block[:, None], positions[None, :], 0), axis=1
    )
    hold_grp = (holder // n_blk).reshape(n_grp, n_blk)
    hold_blk = (holder % n_blk).reshape(n_grp, n_blk)
    own_hold = lax.dynamic_index_in_dim(holder, own_index, 0, keepdims=False)
    own_grp = own_hold // n_blk
    own_query = lax.dynamic_index_in_dim(held_block, own_index, 0, keepdims=False)
    own_key = lax.dynamic_index_in_dim(key_block, own_index, 0, keepdims=False)
    diag = own_query == own_key
    kv_local = jnp.concatenate([key_rows, value_rows], axis=1)
    col_grp = lax.dynamic_index_in_dim(hold_grp, b_index, 1, keepdims=False)
    col_blk = lax.dynamic_index_in_dim(hold_blk, b_index, 1, keepdims=False)
    slots = jnp.arange(n_blk, dtype=jnp.int32)
    select = jnp.logical_and(
        (col_grp == g_index)[:, None], col_blk[:, None] == slots[None, :]
    ).astype(jnp.bfloat16)
    gathered = lax.all_gather(kv_local[None], "blk", axis=0, tiled=True)
    outgoing = jnp.einsum(
        "gp,prc->grc", select, gathered, preferred_element_type=jnp.float32
    ).astype(jnp.bfloat16)
    incoming = lax.all_to_all(outgoing, "grp", split_axis=0, concat_axis=0, tiled=True)
    kv_rows = lax.dynamic_index_in_dim(incoming, own_grp, 0, keepdims=False)
    query_grad, pair_term = pair_grads(queries, out_grad, attn_out, log_norm, kv_rows, diag)
    targets = jnp.arange(n_grp, dtype=jnp.int32)
    sending = jnp.where(
        (targets == own_grp)[:, None, None], pair_term[None], jnp.zeros_like(pair_term)[None]
    )
    returned = lax.all_to_all(sending, "grp", split_axis=0, concat_axis=0, tiled=True)
    pooled = jnp.einsum("gp,grc->prc", select, returned, preferred_element_type=jnp.float32)
    summed = lax.psum_scatter(pooled, "blk", scatter_dimension=0, tiled=True)[0]
    summed = summed.astype(jnp.bfloat16)
    return (query_grad, summed[:, : KVH * DH], summed[:, KVH * DH :])


def solution(mesh):
    return jax.shard_map(
        per_device,
        mesh=mesh,
        in_specs=(
            P(("grp", "blk"), None),
            P(("grp", "blk"), None),
            P(("grp", "blk"), None),
            P(("grp", "blk"), None),
            P(("grp", "blk"), None),
            P(("grp", "blk"), None),
            P(),
            P(),
        ),
        out_specs=(P(("grp", "blk"), None), P(("grp", "blk"), None), P(("grp", "blk"), None)),
        check_vma=False,
    )
```

profile of v0, /device:TPU:15, one launch (start us, length us, event | category | flops | bytes accessed | tf_op | source)
XLA Modules:
  0.0 383.9 jit_solution(11191048178762989151)
XLA Ops:
  10.5 25.7 %all-gather.3.cloned.1.call-done = bf16[2560,512]{1,0:T(8,128)(2,1)} async-done(((bf16[640,512]{1,0:T(8,128)(2,1)}), bf16[2560,512]{1,0:T(8,128)(2,1)}) %all-gather.3.cloned.1.call-update) | async-done | bytes 2621456 | tf_op jit(solution)/shard_map/all_gather | solution.py:73
  36.2 8.4 %convolution_convert_fusion = bf16[8,640,512]{2,0,1:T(8,128)(2,1)S(1)} fusion(bf16[4,640,512]{2,1,0:T(8,128)(2,1)} %bitcast.129, s32[8]{0:T(128)S(1)} %dynamic-slice_reduce_fusion, pred[8]{0:T(512)(128)(4,1)S(1)} %fusion.39), kind=kOutput, calls=%fused_computation.24 | convolution fusion | flops 23593024 | bytes 7864360 | tf_op jit(solution)/shard_map/gp,prc->grc/dot_general | solution.py:74
  44.7 4.2 %copy.58 = bf16[8,640,512]{2,1,0:T(8,128)(2,1)} copy(bf16[8,640,512]{2,0,1:T(8,128)(2,1)S(1)} %convolution_convert_fusion) | data formatting | bytes 10485760 | tf_op jit(solution)/shard_map/convert_element_type | solution.py:76
  48.9 5.6 %all-to-all-start = ((bf16[8,640,512]{2,1,0:T(8,128)(2,1)}), bf16[8,640,512]{2,1,0:T(8,128)(2,1)}, u32[]{:S(2)}, u32[]{:S(2)}) async-start(bf16[8,640,512]{2,1,0:T(8,128)(2,1)} %copy.58), calls=%async_computation | async-start | bytes 10485760 | tf_op jit(solution)/shard_map/all_to_all | solution.py:77
  60.2 3.6 fusion.50
  63.8 2.4 copy.96
  66.2 2.4 copy.98
  70.4 2.5 copy.97
  72.9 2.4 copy.99
  75.3 2.7 multiply_bitcast_fusion
  78.1 3.6 copy.100
  81.6 4.0 %reduce_sum.22 = f32[640,16]{1,0:T(8,128)S(1)} reduce(f32[640,16,128]{2,1,0:T(8,128)} %bitcast.122, f32[]{:T(128)} %constant.71.clone.1), dimensions={2}, to_apply=%region_1.2 | reduce | flops 1300480 | bytes 5283844 | tf_op jit(solution)/shard_map/reduce_sum | solution.py:15
  87.0 80.6 %all-to-all-done = bf16[8,640,512]{2,1,0:T(8,128)(2,1)} async-done(((bf16[8,640,512]{2,1,0:T(8,128)(2,1)}), bf16[8,640,512]{2,1,0:T(8,128)(2,1)}, u32[]{:S(2)}, u32[]{:S(2)}) %all-to-all-start) | async-done | bytes 5242912 | tf_op jit(solution)/shard_map/all_to_all | solution.py:77
  170.7 2.7 fusion.30
  173.4 5.2 %fusion.2 = bf16[8,640,640]{1,2,0:T(8,128)(2,1)S(1)} fusion(f32[640,640,8]{1,0,2:T(8,128)S(1)} %fusion.37, bf16[640,8,128]{0,2,1:T(8,128)(2,1)S(1)} %bitcast.133, f32[8,640]{1,0:T(8,128)S(1)} %copy.70, f32[8,640]{1,0:T(8,128)S(1)} %get-tuple-element.12, pred[640,640]{0,1:T(8,128)(4,1)S(1)} %copy-done.7, bf16[640,512]{1,0:T(8,128)(2,1)S(1)} %dynamic-slice_bitcast_fusion), kind=kOutput, calls=%fused_computation.3 | convolution fusion | flops 861798400 | bytes 21585920 | tf_op jit(solution)/shard_map/igd,jd->gij/dot_general | solution.py:35
  182.8 2.7 fusion.33
  185.5 5.0 %fusion.7 = bf16[8,640,640]{1,2,0:T(8,128)(2,1)S(1)} fusion(f32[640,640,8]{1,0,2:T(8,128)S(1)} %fusion.36, bf16[640,8,128]{0,2,1:T(8,128)(2,1)S(1)} %bitcast.131, f32[8,640]{1,0:T(8,128)S(1)} %copy.63, f32[8,640]{1,0:T(8,128)S(1)} %get-tuple-element.11, pred[640,640]{0,1:T(8,128)(4,1)S(1)} %copy-done.7, bf16[640,512]{1,0:T(8,128)(2,1)S(1)} %dynamic-slice_bitcast_fusion), kind=kOutput, calls=%fused_computation.10 | convolution fusion | flops 861798400 | bytes 21585920 | tf_op jit(solution)/shard_map/igd,jd->gij/dot_general | solution.py:35
  190.5 2.7 copy-done.2
  196.1 119.0 %all_to_all.10 = bf16[8,640,512]{2,1,0:T(8,128)(2,1)S(1)} all-to-all(bf16[8,640,512]{2,1,0:T(8,128)(2,1)S(1)} %broadcast_select_fusion), channel_id=1, replica_groups=mesh['grp'=8,'blk'=4] {'grp'}, dimensions={0} | all-to-all | bytes 10485760 | tf_op jit(solution)/shard_map/all_to_all | solution.py:84
  315.1 3.4 fusion.18
  318.5 3.9 %copy.81 = f32[4,640,512]{2,1,0:T(8,128)} copy(f32[4,640,512]{2,0,1:T(4,128)S(1)} %fusion.18) | data formatting | bytes 10485760 | tf_op jit(solution)/shard_map/gp,grc->prc/dot_general | solution.py:85
  322.4 4.1 %convolution_convert_fusion.1 = bf16[128,8,640]{2,0,1:T(8,128)(2,1)S(1)} fusion(bf16[8,640,640]{1,2,0:T(8,128)(2,1)} %copy-done.1, bf16[640,512]{1,0:T(8,128)(2,1)S(1)} %dynamic-slice_bitcast_fusion), kind=kOutput, calls=%fused_computation.29 | convolution fusion | flops 839516160 | bytes 8028160 | tf_op jit(solution)/shard_map/gij,jd->igd/dot_general | solution.py:38
  327.2 5.1 %convolution_convert_fusion.2 = bf16[128,8,640]{2,0,1:T(8,128)(2,1)} fusion(bf16[8,640,640]{1,2,0:T(8,128)(2,1)} %copy-done.2, bf16[640,512]{1,0:T(8,128)(2,1)S(1)} %dynamic-slice_bitcast_fusion), kind=kOutput, calls=%fused_computation.30 | convolution fusion | flops 839516160 | bytes 8028160 | tf_op jit(solution)/shard_map/gij,jd->igd/dot_general | solution.py:38
  335.8 39.0 %reduce-scatter.2.cloned.1.call-done = f32[1,640,512]{2,1,0:T(8,128)} async-done(((f32[4,640,512]{2,1,0:T(8,128)}), f32[1,640,512]{2,1,0:T(8,128)}) %reduce-scatter.2.cloned.1.call-update) | async-done | bytes 1310736 | tf_op jit(solution)/shard_map/reduce_scatter | solution.py:86
  (54 shorter events, 24.7 us)
Async XLA Ops:
  7.2 29.1 %all-gather.3.cloned.1.call-start = ((), (), s32[]{:S(2)}) async-start(), calls=%async_computation.4 | async-start | bytes 3276800 | tf_op jit(solution)/shard_map/all_gather | solution.py:73
  48.9 5.6 %copy-start.9 = (s32[32]{0:T(128)S(1)}, s32[32]{0:T(128)}, u32[]{:S(2)}) copy-start(s32[32]{0:T(128)} %param.15) | copy-start | bytes 388
  48.9 6.2 %copy-start.10 = (s32[32]{0:T(128)S(1)}, s32[32]{0:T(128)}, u32[]{:S(2)}) copy-start(s32[32]{0:T(128)} %param.14) | copy-start | bytes 388
  48.9 118.7 %all-to-all-start = ((bf16[8,640,512]{2,1,0:T(8,128)(2,1)}), bf16[8,640,512]{2,1,0:T(8,128)(2,1)}, u32[]{:S(2)}, u32[]{:S(2)}) async-start(bf16[8,640,512]{2,1,0:T(8,128)(2,1)} %copy.58), calls=%async_computation | async-start | bytes 10485760 | tf_op jit(solution)/shard_map/all_to_all | solution.py:77
  54.5 320.3 %reduce-scatter.2.cloned.1.call-start = ((), (), s32[]{:S(2)}) async-start(), calls=%async_computation.3 | async-start | bytes 6553600 | tf_op jit(solution)/shard_map/reduce_scatter | solution.py:86
  60.2 8.5 %copy-start = (bf16[640,2048]{1,0:T(8,128)(2,1)S(1)}, bf16[640,2048]{1,0:T(8,128)(2,1)}, u32[]{:S(2)}) copy-start(bf16[640,2048]{1,0:T(8,128)(2,1)} %param.11) | copy-start | bytes 7864324
  81.6 5.4 %copy-start.8 = (f32[640,16]{0,1:T(8,128)S(1)}, f32[640,16]{0,1:T(8,128)}, u32[]{:S(2)}) copy-start(f32[640,16]{0,1:T(8,128)} %param.13) | copy-start | bytes 122884
  81.6 87.1 %copy-start.4 = (bf16[640,1024]{0,1:T(8,128)(2,1)S(1)}, bf16[640,1024]{0,1:T(8,128)(2,1)}, u32[]{:S(2)}) copy-start(bf16[640,1024]{0,1:T(8,128)(2,1)} %copy.98) | copy-start | bytes 3932164
  168.8 1.9 copy-start.6
  168.8 1.9 copy-start.7
  178.6 4.2 %copy-start.1 = (bf16[8,640,640]{1,2,0:T(8,128)(2,1)}, bf16[8,640,640]{1,2,0:T(8,128)(2,1)S(1)}, u32[]{:S(2)}) copy-start(bf16[8,640,640]{1,2,0:T(8,128)(2,1)S(1)} %fusion.2) | copy-start | bytes 19660804
  178.6 2.3 copy-start.3
  180.9 1.9 copy-start.5
  190.4 2.7 copy-start.2
Sparse Core Ops, SparseCore 0:
  10.1 26.0 all-gather.2
  322.5 52.2 reduce-scatter.1
where the time goes:
time: 387 us; the launch traced here: 384 us
  waiting for transfers between devices  145 us (37%)
  blocking collectives  119 us (31%)
  matrix products  44.6 us (12%)
  local copies, waits for them, and re-layouts  36.8 us (10%)
  between operations  18.2 us (5%)
  other arithmetic  14.4 us (4%)
  starting transfers between devices  5.65 us (1%)
    all_to_all x1, blocking collectives, per_device(): lax.all_to_all(sending, 'grp', split_axis=0, concat_axis=0, tiled=True)  119 us
    all_to_all x1, waiting for transfers between devices, per_device(): lax.all_to_all(outgoing, 'grp', split_axis=0, concat_axis=0, tiled=True)  80.6 us
    reduce_scatter x1, waiting for transfers between devices, per_device(): summed = lax.psum_scatter(pooled, 'blk', scatter_dimension=0, tiled=True)[0]  39 us
    all_gather x1, waiting for transfers between devices, per_device(): gathered = lax.all_gather(kv_local[None], 'blk', axis=0, tiled=True)  25.7 us
    unnamed x27, local copies, waits for them, and re-layouts  16.2 us
    dot_general x2, matrix products, pair_grads(): jnp.einsum('igd,jd->gij', o_head, v_head, preferred_element_type=jnp.floa...  10.2 us
    dot_general x2, matrix products, pair_grads(): jnp.einsum('gij,jd->igd', dscore, k_head, preferred_element_type=jnp.floa...  9.22 us
    dot_general x1, matrix products, per_device(): jnp.einsum('gp,prc->grc', select, gathered, preferred_element_type=jnp.fl...  8.43 us
  transfers between devices with their start and end apart: 3, of which 3 were waited for; matrix products, arithmetic and copies ran while one was open for 11% of the time, Pallas kernels for 0%

commit v1 on v0

v1 whole, which is shorter than its diff:
```python
import functools

import jax
import jax.numpy as jnp
from jax import lax
from jax.experimental import pallas as pl
from jax.experimental.pallas import tpu as pltpu

H = 16
KVH = 2
DH = 128
GROUP = H // KVH
SCALE = DH ** (-0.5)
LOG2E = 1.4426950408889634
MESH = pl.DeviceIdType.MESH


def chunks_of(rows, width):
    return [(at, min(width, rows - at)) for at in range(0, rows, width)]


def plan_kernel(n, held_ref, key_ref, plan_ref, inv, count):
    def zero(e, c):
        count[e] = 0
        return c

    def invert(e, c):
        inv[held_ref[e]] = e
        return c

    def hold(d, c):
        e = inv[key_ref[d]]
        plan_ref[d] = e
        count[e] = count[e] + 1
        return c

    def prefix(e, at):
        many = count[e]
        count[e] = at
        plan_ref[3 * n + e] = jnp.maximum(at + many - 1, 0)
        plan_ref[4 * n + e] = jnp.minimum(many, 1)
        return at + many

    def place(d, c):
        e = plan_ref[d]
        at = count[e]
        plan_ref[n + at] = d
        plan_ref[2 * n + at] = inv[e]
        inv[e] = 1
        count[e] = at + 1
        return c

    def clear(e, c):
        inv[e] = 0
        return c

    lax.fori_loop(0, n, zero, 0)
    lax.fori_loop(0, n, invert, 0)
    lax.fori_loop(0, n, hold, 0)
    lax.fori_loop(0, n, prefix, 0)
    lax.fori_loop(0, n, clear, 0)
    lax.fori_loop(0, n, place, 0)


def make_plan(n, held_block, key_block):
    return pl.pallas_call(
        functools.partial(plan_kernel, n),
        out_shape=jax.ShapeDtypeStruct((5 * n,), jnp.int32),
        in_specs=[pl.BlockSpec(memory_space=pltpu.SMEM)] * 2,
        out_specs=pl.BlockSpec(memory_space=pltpu.SMEM),
        scratch_shapes=[pltpu.SMEM((n,), jnp.int32), pltpu.SMEM((n,), jnp.int32)],
    )(held_block, key_block)


def own_place():
    return lax.axis_index("grp") * lax.axis_size("blk") + lax.axis_index("blk")


def meet_all(n, n_blk, me):
    barrier = pltpu.get_barrier_semaphore()

    def greet(k, c):
        t = lax.rem(me + k, n)
        pl.semaphore_signal(
            barrier, inc=1, device_id=(t // n_blk, lax.rem(t, n_blk)), device_id_type=MESH
        )
        return c

    lax.fori_loop(1, n, greet, 0)
    pl.semaphore_wait(barrier, n - 1)


def start_exchange(n, n_blk, me, src, dst, send_sem, recv_sem):
    def push(k, c):
        t = lax.rem(me + k, n)
        pltpu.make_async_remote_copy(
            src_ref=src.at[t],
            dst_ref=dst.at[me],
            send_sem=send_sem,
            recv_sem=recv_sem,
            device_id=(t // n_blk, lax.rem(t, n_blk)),
            device_id_type=MESH,
        ).start()
        return c

    lax.fori_loop(1, n, push, 0)


def wait_bytes(n, ref, sem):
    part = ref.at[pl.ds(0, n - 1)]
    pltpu.make_async_copy(part, part, sem).wait()


def fetch_kernel(n, n_blk, plan_ref, kv_ref, out_ref, held, picked, sems):
    me = own_place()
    meet_all(n, n_blk, me)
    start_exchange(n, n_blk, me, kv_ref, held, sems.at[0], sems.at[1])
    held[me] = kv_ref[me]
    wait_bytes(n, held, sems.at[1])

    def pick(d, c):
        picked[d] = held[plan_ref[d]]
        return c

    lax.fori_loop(0, n, pick, 0)
    start_exchange(n, n_blk, me, picked, out_ref, sems.at[2], sems.at[3])
    out_ref[me] = picked[me]
    wait_bytes(n, kv_ref, sems.at[0])
    wait_bytes(n, picked, sems.at[2])
    wait_bytes(n, out_ref, sems.at[3])


def return_kernel(n, n_blk, plan_ref, pair_ref, out_ref, terms, sums, picked, sems):
    me = own_place()
    meet_all(n, n_blk, me)
    start_exchange(n, n_blk, me, pair_ref, terms, sems.at[0], sems.at[1])
    terms[me] = pair_ref[me]
    wait_bytes(n, terms, sems.at[1])

    def add(k, total):
        term = terms[plan_ref[n + k]].astype(jnp.float32)
        total = jnp.where(plan_ref[2 * n + k] == 1, total, 0.0) + term
        sums[k] = total
        return total

    lax.fori_loop(0, n, add, jnp.zeros(sums.shape[1:], jnp.float32))

    def pick(e, c):
        total = sums[plan_ref[3 * n + e]]
        picked[e] = jnp.where(plan_ref[4 * n + e] == 1, total, 0.0).astype(jnp.bfloat16)
        return c

    lax.fori_loop(0, n, pick, 0)
    start_exchange(n, n_blk, me, picked, out_ref, sems.at[2], sems.at[3])
    out_ref[me] = picked[me]
    wait_bytes(n, pair_ref, sems.at[0])
    wait_bytes(n, picked, sems.at[2])
    wait_bytes(n, out_ref, sems.at[3])


def exchange_call(kernel, n, n_blk, plan, pieces, scratch, collective_id):
    vmem = pl.BlockSpec(memory_space=pltpu.VMEM)
    return pl.pallas_call(
        functools.partial(kernel, n, n_blk),
        out_shape=jax.ShapeDtypeStruct(pieces.shape, jnp.bfloat16),
        in_specs=[pl.BlockSpec(memory_space=pltpu.SMEM), vmem],
        out_specs=vmem,
        scratch_shapes=scratch + [pltpu.SemaphoreType.DMA((4,))],
        compiler_params=pltpu.CompilerParams(collective_id=collective_id, has_side_effects=True),
    )(plan, pieces)


NT = (((1,), (1,)), ((), ()))
TN = (((0,), (0,)), ((), ()))


def pair_kernel(width, diag_ref, lse_ref, q_ref, do_ref, o_ref, k_ref, v_ref, dq_ref, pair_ref, dk_acc, dv_acc):
    head = pl.program_id(0)
    rows = q_ref.shape[0]
    step = lax.rem(head, GROUP)

    @pl.when(step == 0)
    def _():
        dk_acc[...] = jnp.zeros_like(dk_acc)
        dv_acc[...] = jnp.zeros_like(dv_acc)

    def body(diag):
        for at, w in chunks_of(rows, width):
            keys = min(rows, at + w) if diag else rows
            q = q_ref[at : at + w, :]
            do = do_ref[at : at + w, :]
            o = o_ref[at : at + w, :]
            k = k_ref[0, :keys, :]
            v = v_ref[0, :keys, :]
            lse = lse_ref[0, :, at : at + w] * LOG2E
            prod = do.astype(jnp.float32) * o.astype(jnp.float32)
            delta = jnp.sum(jnp.transpose(prod), axis=0, keepdims=True)
            s = lax.dot_general(k, q, NT, preferred_element_type=jnp.float32)
            p = jnp.exp2(s * (SCALE * LOG2E) - lse)
            if diag:
                j = lax.broadcasted_iota(jnp.int32, p.shape, 0)
                i = lax.broadcasted_iota(jnp.int32, p.shape, 1) + at
                p = jnp.where(j <= i, p, 0.0)
            dp = lax.dot_general(v, do, NT, preferred_element_type=jnp.float32)
            ds = (p * (dp - delta)).astype(jnp.bfloat16)
            dv_acc[:keys, :] += jnp.dot(
                p.astype(jnp.bfloat16), do, preferred_element_type=jnp.float32
            )
            dk_acc[:keys, :] += jnp.dot(ds, q, preferred_element_type=jnp.float32)
            dq = lax.dot_general(ds, k, TN, preferred_element_type=jnp.float32)
            dq_ref[at : at + w, :] = (dq * SCALE).astype(jnp.bfloat16)

    @pl.when(diag_ref[0] == 1)
    def _():
        body(True)

    @pl.when(diag_ref[0] == 0)
    def _():
        body(False)

    @pl.when(step == GROUP - 1)
    def _():
        pair_ref[0, 0] = (dk_acc[...] * SCALE).astype(jnp.bfloat16)
        pair_ref[1, 0] = dv_acc[...].astype(jnp.bfloat16)


def pair_grads(queries, out_grad, attn_out, lse, kv, diag, width=256):
    rows = queries.shape[0]
    col = pl.BlockSpec((rows, DH), lambda h: (0, h))
    return pl.pallas_call(
        functools.partial(pair_kernel, width),
        out_shape=(
            jax.ShapeDtypeStruct((rows, H * DH), jnp.bfloat16),
            jax.ShapeDtypeStruct((2, KVH, rows, DH), jnp.bfloat16),
        ),
        grid=(H,),
        in_specs=[
            pl.BlockSpec(memory_space=pltpu.SMEM),
            pl.BlockSpec((1, 1, rows), lambda h: (h, 0, 0)),
            col,
            col,
            col,
            pl.BlockSpec((1, rows, DH), lambda h: (h // GROUP, 0, 0)),
            pl.BlockSpec((1, rows, DH), lambda h: (KVH + h // GROUP, 0, 0)),
        ],
        out_specs=(col, pl.BlockSpec((2, 1, rows, DH), lambda h: (0, h // GROUP, 0, 0))),
        scratch_shapes=[pltpu.VMEM((rows, DH), jnp.float32)] * 2,
        compiler_params=pltpu.CompilerParams(dimension_semantics=("arbitrary",)),
    )(diag, lse, queries, out_grad, attn_out, kv, kv)


def split_heads(rows_array):
    return [rows_array[:, c * DH : (c + 1) * DH] for c in range(KVH)]


def per_device(queries, key_rows, value_rows, out_grad, attn_out, log_norm, held_block, key_block):
    n_blk = lax.axis_size("blk")
    n = lax.axis_size("grp") * n_blk
    rows = queries.shape[0]
    me = own_place()
    part = 2 * KVH * rows // n
    piece = (n, part, DH)
    diag = (
        lax.dynamic_slice_in_dim(held_block, me, 1) == lax.dynamic_slice_in_dim(key_block, me, 1)
    ).astype(jnp.int32)
    plan = make_plan(n, held_block, key_block)
    kv_own = jnp.stack(split_heads(key_rows) + split_heads(value_rows)).reshape(piece)
    buf = pltpu.VMEM(piece, jnp.bfloat16)
    kv = exchange_call(fetch_kernel, n, n_blk, plan, kv_own, [buf, buf], 0)
    kv = kv.reshape(2 * KVH, rows, DH)
    lse = jnp.transpose(log_norm)[:, None, :]
    query_grad, pair = pair_grads(queries, out_grad, attn_out, lse, kv, diag)
    grads = exchange_call(
        return_kernel, n, n_blk, plan, pair.reshape(piece),
        [buf, pltpu.VMEM(piece, jnp.float32), buf], 1,
    )
    grads = grads.reshape(2, KVH, rows, DH)
    key_grad = jnp.concatenate([grads[0, c] for c in range(KVH)], axis=1)
    value_grad = jnp.concatenate([grads[1, c] for c in range(KVH)], axis=1)
    return query_grad, key_grad, value_grad


def solution(mesh):
    row = jax.sharding.PartitionSpec(("grp", "blk"), None)
    flat = jax.sharding.PartitionSpec()
    return jax.shard_map(
        per_device,
        mesh=mesh,
        in_specs=(row, row, row, row, row, row, flat, flat),
        out_specs=(row, row, row),
        check_vma=False,
    )
```

time: 387 us -> 116 us (0.30)
  waiting for transfers between devices: 145 us -> 0 us
  blocking collectives: 119 us -> 0 us
  Pallas kernels: 0 us -> 105 us
  matrix products: 44.6 us -> 0 us
  local copies, waits for them, and re-layouts: 36.8 us -> 6.3 us
  between operations: 18.2 us -> 1.97 us
  other arithmetic: 14.4 us -> 2.44 us
  starting transfers between devices: 5.65 us -> 0 us
    all_to_all x1 -> x0, blocking collectives: 119 us -> none  [per_device(): lax.all_to_all(sending, 'grp', split_axis=0, concat_axis=0, tiled=True)]
    pallas_call x0 -> x4, Pallas kernels: none -> 105 us  [the longest x2 76.1 us: exchange_call(): pl.pallas_call(functools.partial(kernel, n, n_blk), out_shape=jax.ShapeDt...]
    all_to_all x1 -> x0, waiting for transfers between devices: 80.6 us -> none  [per_device(): lax.all_to_all(outgoing, 'grp', split_axis=0, concat_axis=0, tiled=True)]
    dot_general x12 -> x0, matrix products: 44.6 us -> none  [the longest x2 10.2 us: pair_grads(): jnp.einsum('igd,jd->gij', o_head, v_head, preferred_element_type=jnp.floa...]
    reduce_scatter x1 -> x0, waiting for transfers between devices: 39 us -> none  [per_device(): summed = lax.psum_scatter(pooled, 'blk', scatter_dimension=0, tiled=True)[0]]
    all_gather x1 -> x0, waiting for transfers between devices: 25.7 us -> none  [per_device(): gathered = lax.all_gather(kv_local[None], 'blk', axis=0, tiled=True)]
    unnamed x27 -> x0, local copies, waits for them, and re-layouts: 16.2 us -> none
    slice x3 -> x0, local copies, waits for them, and re-layouts: 6.28 us -> none  [the longest x1 3.62 us: pair_grads(): q_head = query[:, head * width:(head + 1) * width].reshape(rows, group, DH)]
  transfers between devices with their start and end apart: 3 -> 0, of which waited for: 3 -> 0; matrix products, arithmetic and copies ran while one was open for 11% -> 0% of each run, Pallas kernels for 0% -> 0%
where the time goes in v1:
time: 116 us; the launch traced here: 115 us
  Pallas kernels  105 us (91%)
  local copies, waits for them, and re-layouts  6.3 us (5%)
  other arithmetic  2.44 us (2%)
  between operations  1.97 us (2%)
    pallas_call x2, Pallas kernels, exchange_call(): pl.pallas_call(functools.partial(kernel, n, n_blk), out_shape=jax.ShapeDt...  76.1 us
    pallas_call x1, Pallas kernels, pair_grads(): pl.pallas_call(functools.partial(pair_kernel, width), out_shape=(jax.Shap...  25.5 us
    pallas_call x1, Pallas kernels, make_plan(): pl.pallas_call(functools.partial(plan_kernel, n), out_shape=jax.ShapeDtyp...  2.97 us

profile of v1, /device:TPU:15, one launch (start us, length us, event | category | flops | bytes accessed | tf_op | source)
XLA Modules:
  0.0 115.3 jit_solution(15451378994899753544)
XLA Ops:
  0.6 1.2 %dynamic_slice.7 = s32[1]{0:T(128)} dynamic-slice(s32[32]{0:T(128)} %key_ref.1, s32[]{:T(128)S(6)} %select_n.4), dynamic_slice_sizes={1} | dynamic-slice | bytes 12 | tf_op jit(solution)/shard_map/dynamic_slice | solution.py:264
  1.9 1.2 %dynamic_slice.6 = s32[1]{0:T(128)} dynamic-slice(s32[32]{0:T(128)} %held_ref.1, s32[]{:T(128)S(6)} %select_n.4), dynamic_slice_sizes={1} | dynamic-slice | bytes 12 | tf_op jit(solution)/shard_map/dynamic_slice | solution.py:264
  4.4 3.0 %shard_map.103.plan_ref = s32[160]{0:T(256)} custom-call(s32[32]{0:T(128)} %held_ref.1, s32[32]{0:T(128)} %key_ref.1), custom_call_target="tpu_custom_call" | custom-call | tf_op jit(solution)/shard_map/pallas_call | solution.py:66
  7.4 1.4 %broadcast_in_dim.3.lse_ref = f32[16,1,640]{2,1,0:T(1,128)} reshape(f32[16,640]{1,0:T(8,128)} %bitcast.26) | data formatting | bytes 81920 | tf_op jit(solution)/shard_map/broadcast_in_dim | solution.py:271
  8.8 1.2 %slice_bitcast_fusion.5 = (bf16[1,640,128]{2,1,0:T(8,128)(2,1)S(1)}, bf16[1,640,128]{2,1,0:T(8,128)(2,1)S(1)}, bf16[1,640,128]{2,1,0:T(8,128)(2,1)S(1)}, bf16[1,640,128]{2,1,0:T(8,128)(2,1)S(1)}) fusion(bf16[640,256]{1,0:T(8,128)(2,1)} %param.10, bf16[640,256]{1,0:T(8,128)(2,1)} %param.9), kind=kLoop, calls=%fused_computation.8 | loop fusion | bytes 1310720 | tf_op jit(solution)/shard_map/stack | solution.py:267
  10.0 0.9 pad_maximum_fusion
  10.9 37.8 %shard_map.104 = bf16[32,80,128]{2,1,0:T(8,128)(2,1)} custom-call(s32[160]{0:T(256)} %shard_map.103.plan_ref, bf16[32,80,128]{2,1,0:T(8,128)(2,1)} %bitcast.24), custom_call_target="tpu_custom_call" | custom-call | tf_op jit(solution)/shard_map/pallas_call | solution.py:163
  48.7 25.5 %shard_map.105 = (bf16[640,2048]{1,0:T(8,128)(2,1)}, bf16[2,2,640,128]{3,2,1,0:T(8,128)(2,1)}) custom-call(s32[1]{0:T(128)S(6)} %convert_element_type.3.diag_ref, f32[16,1,640]{2,1,0:T(1,128)} %broadcast_in_dim.3.lse_ref, bf16[640,2048]{1,0:T(8,128)(2,1)} %q_ref.1, bf16[640,2048]{1,0:T(8,128)(2,1)} %do_ref.1, bf16[640,2048]{1,0:T(8,128)(2,1)} %o_ref.1, ...), custom_call_target="tpu_custom_call" | custom-call | tf_op jit(solution)/shard_map/pallas_call | solution.py:230
  74.2 38.3 %shard_map.106 = bf16[32,80,128]{2,1,0:T(8,128)(2,1)} custom-call(s32[160]{0:T(256)} %shard_map.103.plan_ref, bf16[32,80,128]{2,1,0:T(8,128)(2,1)} %bitcast.25), custom_call_target="tpu_custom_call" | custom-call | tf_op jit(solution)/shard_map/pallas_call | solution.py:163
  112.6 1.2 %slice_bitcast_fusion.1 = (bf16[640,128]{1,0:T(8,128)(2,1)S(1)}, bf16[640,128]{1,0:T(8,128)(2,1)S(1)}, bf16[640,128]{1,0:T(8,128)(2,1)S(1)}, bf16[640,128]{1,0:T(8,128)(2,1)S(1)}) fusion(bf16[2,2,640,128]{3,2,1,0:T(8,128)(2,1)} %bitcast.23), kind=kLoop, calls=%fused_computation.4 | loop fusion | bytes 1310720 | tf_op jit(solution)/shard_map/squeeze | solution.py:279
  113.8 0.8 pad_maximum_fusion.2
  114.5 0.8 pad_maximum_fusion.1

commit v2 on v1

v2 whole, which is shorter than its diff:
```python
import functools

import jax
import jax.numpy as jnp
from jax import lax
from jax.experimental import pallas as pl
from jax.experimental.pallas import tpu as pltpu

H = 16
KVH = 2
DH = 128
GROUP = H // KVH
SCALE = DH ** (-0.5)
LOG2E = 1.4426950408889634
MESH = pl.DeviceIdType.MESH


def chunks_of(rows, width):
    return [(at, min(width, rows - at)) for at in range(0, rows, width)]


def plan_kernel(n, held_ref, key_ref, plan_ref, inv, count):
    def zero(e, c):
        count[e] = 0
        return c

    def invert(e, c):
        inv[held_ref[e]] = e
        return c

    def hold(d, c):
        e = inv[key_ref[d]]
        plan_ref[d] = e
        count[e] = count[e] + 1
        return c

    def prefix(e, at):
        many = count[e]
        count[e] = at
        plan_ref[3 * n + e] = jnp.maximum(at + many - 1, 0)
        plan_ref[4 * n + e] = jnp.minimum(many, 1)
        return at + many

    def place(d, c):
        e = plan_ref[d]
        at = count[e]
        plan_ref[n + at] = d
        plan_ref[2 * n + at] = inv[e]
        inv[e] = 1
        count[e] = at + 1
        return c

    def clear(e, c):
        inv[e] = 0
        return c

    me = own_place()
    plan_ref[5 * n] = jnp.where(held_ref[me] == key_ref[me], 1, 0)
    lax.fori_loop(0, n, zero, 0)
    lax.fori_loop(0, n, invert, 0)
    lax.fori_loop(0, n, hold, 0)
    lax.fori_loop(0, n, prefix, 0)
    lax.fori_loop(0, n, clear, 0)
    lax.fori_loop(0, n, place, 0)


def make_plan(n, held_block, key_block):
    return pl.pallas_call(
        functools.partial(plan_kernel, n),
        out_shape=jax.ShapeDtypeStruct((5 * n + 1,), jnp.int32),
        in_specs=[pl.BlockSpec(memory_space=pltpu.SMEM)] * 2,
        out_specs=pl.BlockSpec(memory_space=pltpu.SMEM),
        scratch_shapes=[pltpu.SMEM((n,), jnp.int32), pltpu.SMEM((n,), jnp.int32)],
    )(held_block, key_block)


def own_place():
    return lax.axis_index("grp") * lax.axis_size("blk") + lax.axis_index("blk")


NT = (((1,), (1,)), ((), ()))
TN = (((0,), (0,)), ((), ()))
FAR = 1e30


def fused_kernel(
    n, n_blk, m, width, plan_ref, kv_ref, lse_ref, q_hbm, do_hbm, o_hbm,
    dq_hbm, out_ref,
    q_ref, do_ref, o_ref, dq_ref, lse3, delta3, held, picked, kv, pair, terms, sums, sent,
    dk_acc, dv_acc, sems, local_sems,
):
    rows = q_ref.shape[0]
    half = m // 2
    me = own_place()
    kind = lax.rem(me, 2)
    slot = kind * half + me // 2
    relay = me < m
    fetch_in, fetch_out, return_in, return_out = [sems.at[i] for i in range(4)]
    kv_out, kv_in, pair_out, grad_in = [(sems.at[i], sems.at[i + 1]) for i in range(4, 12, 2)]
    place = lambda t: (t // n_blk, lax.rem(t, n_blk))

    loads = [
        pltpu.make_async_copy(src, dst, local_sems.at[i])
        for i, (src, dst) in enumerate(((do_hbm, do_ref), (o_hbm, o_ref), (q_hbm, q_ref)))
    ]
    barrier = pltpu.get_barrier_semaphore()

    def greet(k, c):
        pl.semaphore_signal(
            barrier, inc=1, device_id=place(lax.rem(me + k, n)), device_id_type=MESH
        )
        return c

    lax.fori_loop(1, n, greet, 0)
    for load in loads:
        load.start()
    pl.semaphore_wait(barrier, n - 1)

    def to_relays(c, src, dst, send_sem, recv_sem):
        def push(k, carry):
            at = lax.rem(me // 2 + k, half)
            t = 2 * at + c

            @pl.when(t != me)
            def _():
                pltpu.make_async_remote_copy(
                    src_ref=src.at[c * half + at], dst_ref=dst.at[me],
                    send_sem=send_sem, recv_sem=recv_sem,
                    device_id=place(t), device_id_type=MESH,
                ).start()

            return carry

        lax.fori_loop(0, half, push, 0)

        @pl.when(jnp.logical_and(relay, kind == c))
        def _():
            dst[me] = src[slot]

    def from_relay(src, dst, send_sem, recv_sem):
        def push(k, carry):
            t = lax.rem(me + k, n)
            pltpu.make_async_remote_copy(
                src_ref=src.at[t], dst_ref=dst.at[slot],
                send_sem=send_sem, recv_sem=recv_sem,
                device_id=place(t), device_id_type=MESH,
            ).start()
            return carry

        lax.fori_loop(1, n, push, 0)
        dst[slot] = src[me]

    def wait(ref, count, sem):
        part = ref.at[pl.ds(0, count)]
        pltpu.make_async_copy(part, part, sem).wait()

    def wait_pieces(c, ref, sem):
        mine = jnp.logical_and(relay, kind == c)

        @pl.when(mine)
        def _():
            wait(ref, half - 1, sem)

        @pl.when(jnp.logical_not(mine))
        def _():
            wait(ref, half, sem)

    def on_relay(c, work):
        @pl.when(jnp.logical_and(relay, kind == c))
        def _():
            work(c)

    def deliver(c):
        wait(held, n - 1, fetch_in)

        def pick(d, carry):
            picked[d] = held[plan_ref[d]]
            return carry

        lax.fori_loop(0, n, pick, 0)
        from_relay(picked, kv, fetch_out, kv_in[c])

    def settle(c):
        wait(terms, n - 1, return_in)

        def add(k, total):
            term = terms[plan_ref[n + k]].astype(jnp.float32)
            total = jnp.where(plan_ref[2 * n + k] == 1, total, 0.0) + term
            sums[k] = total
            return total

        lax.fori_loop(0, n, add, jnp.zeros(sums.shape[1:], jnp.float32))

        def pick(e, carry):
            total = sums[plan_ref[3 * n + e]]
            sent[e] = jnp.where(plan_ref[4 * n + e] == 1, total, 0.0).astype(jnp.bfloat16)
            return carry

        lax.fori_loop(0, n, pick, 0)
        from_relay(sent, out_ref, return_out, grad_in[c])

    def heads(c, first, last):
        diag = plan_ref[5 * n]
        slack = rows * (1 - diag)

        def one(h, carry):
            col = pl.ds(pl.multiple_of(h * DH, DH), DH)
            k = kv[c * half : c * half + half // 2].reshape(rows, DH)
            v = kv[c * half + half // 2 : (c + 1) * half].reshape(rows, DH)
            dk, dv = dk_acc[...], dv_acc[...]
            for at, w in chunks_of(rows, width):
                q = q_ref[at : at + w, col]
                do = do_ref[at : at + w, col]
                lse = lse3[h, :, at : at + w]
                delta = delta3[h, :, at : at + w]
                s = lax.dot_general(k, q, NT, preferred_element_type=jnp.float32)
                s = s * (SCALE * LOG2E)
                parts = []
                if at:
                    parts.append(jnp.exp2(s[:at] - lse))
                square = jnp.exp2(s[at : at + w] - lse)
                j = lax.broadcasted_iota(jnp.int32, square.shape, 0)
                i = lax.broadcasted_iota(jnp.int32, square.shape, 1)
                parts.append(jnp.where(j - i <= slack, square, 0.0))
                if at + w < rows:
                    parts.append(jnp.exp2(s[at + w :] - jnp.where(diag == 1, FAR, lse)))
                p = jnp.concatenate(parts, axis=0)
                dp = lax.dot_general(v, do, NT, preferred_element_type=jnp.float32)
                ds = (p * (dp - delta)).astype(jnp.bfloat16)
                dv = dv + jnp.dot(p.astype(jnp.bfloat16), do, preferred_element_type=jnp.float32)
                dk = dk + jnp.dot(ds, q, preferred_element_type=jnp.float32)
                dq = lax.dot_general(ds, k, TN, preferred_element_type=jnp.float32)
                dq_ref[at : at + w, col] = (dq * SCALE).astype(jnp.bfloat16)
            dk_acc[...] = dk
            dv_acc[...] = dv
            return carry

        lax.fori_loop(first, last, one, 0)

    def clear():
        dk_acc[...] = jnp.zeros_like(dk_acc)
        dv_acc[...] = jnp.zeros_like(dv_acc)

    def store_pair(c):
        shape = (half // 2,) + pair.shape[1:]
        pair[c * half : c * half + half // 2] = (
            (dk_acc[...] * SCALE).astype(jnp.bfloat16).reshape(shape)
        )
        pair[c * half + half // 2 : (c + 1) * half] = (
            dv_acc[...].astype(jnp.bfloat16).reshape(shape)
        )

    to_relays(0, kv_ref, held, kv_out[0], fetch_in)
    for h in range(H):
        lse3[h] = lse_ref[h : h + 1, :] * LOG2E
    loads[0].wait()
    loads[1].wait()

    def make_delta(h, carry):
        col = pl.ds(pl.multiple_of(h * DH, DH), DH)
        prod = do_ref[:, col].astype(jnp.float32) * o_ref[:, col].astype(jnp.float32)
        delta3[h] = jnp.sum(jnp.transpose(prod), axis=0, keepdims=True)
        return carry

    lax.fori_loop(0, H, make_delta, 0)
    loads[2].wait()
    first = jnp.logical_and(relay, kind == 0)

    @pl.when(first)
    def _():
        deliver(0)
        to_relays(1, kv_ref, held, kv_out[1], fetch_in)

    wait_pieces(0, kv, kv_in[0])

    @pl.when(jnp.logical_not(first))
    def _():
        to_relays(1, kv_ref, held, kv_out[1], fetch_in)

    clear()
    heads(0, 0, GROUP // 2)
    on_relay(1, deliver)
    heads(0, GROUP // 2, GROUP)
    store_pair(0)
    to_relays(0, pair, terms, pair_out[0], return_in)
    wait_pieces(1, kv, kv_in[1])
    clear()
    heads(1, GROUP, GROUP + GROUP // 2)
    on_relay(0, settle)
    heads(1, GROUP + GROUP // 2, H)
    store_pair(1)
    to_relays(1, pair, terms, pair_out[1], return_in)
    save = pltpu.make_async_copy(dq_ref, dq_hbm, local_sems.at[0])
    save.start()
    on_relay(1, settle)
    for c in range(KVH):
        wait_pieces(c, kv_ref, kv_out[c])
        wait_pieces(c, pair, pair_out[c])
        wait_pieces(c, out_ref, grad_in[c])

    @pl.when(relay)
    def _():
        wait(picked, n - 1, fetch_out)
        wait(sent, n - 1, return_out)

    save.wait()


def relay_count(n, rows):
    fits = [
        m for m in range(4, n + 1, 4)
        if 4 * rows % m == 0 and (4 * rows // m) % 16 == 0 and rows % (4 * rows // m) == 0
    ]
    return max(fits)


def per_device(queries, key_rows, value_rows, out_grad, attn_out, log_norm, held_block, key_block):
    n_blk = lax.axis_size("blk")
    n = lax.axis_size("grp") * n_blk
    rows = queries.shape[0]
    m = relay_count(n, rows)
    part = 2 * KVH * rows // m
    plan = make_plan(n, held_block, key_block)
    cut = lambda x, c: x[:, c * DH : (c + 1) * DH]
    kv_own = jnp.stack([cut(x, c) for c in range(KVH) for x in (key_rows, value_rows)])
    lse = jnp.transpose(log_norm)
    vmem = pl.BlockSpec(memory_space=pltpu.VMEM)
    hbm = pl.BlockSpec(memory_space=pl.ANY)
    wide = pltpu.VMEM((rows, H * DH), jnp.bfloat16)
    line = pltpu.VMEM((H, 1, rows), jnp.float32)
    by_device = pltpu.VMEM((n, part, DH), jnp.bfloat16)
    by_slot = pltpu.VMEM((m, part, DH), jnp.bfloat16)
    acc = pltpu.VMEM((rows, DH), jnp.float32)
    query_grad, grads = pl.pallas_call(
        functools.partial(fused_kernel, n, n_blk, m, 256),
        out_shape=(
            jax.ShapeDtypeStruct((rows, H * DH), jnp.bfloat16),
            jax.ShapeDtypeStruct((m, part, DH), jnp.bfloat16),
        ),
        in_specs=[pl.BlockSpec(memory_space=pltpu.SMEM), vmem, vmem, hbm, hbm, hbm],
        out_specs=(hbm, vmem),
        scratch_shapes=[
            wide, wide, wide, wide, line, line,
            by_device, by_device, by_slot, by_slot, by_device,
            pltpu.VMEM((n, part, DH), jnp.float32), by_device,
            acc, acc, pltpu.SemaphoreType.DMA((12,)), pltpu.SemaphoreType.DMA((3,)),
        ],
        compiler_params=pltpu.CompilerParams(collective_id=0, has_side_effects=True),
    )(plan, kv_own.reshape(m, part, DH), lse, queries, out_grad, attn_out)
    grads = grads.reshape(KVH, 2, rows, DH)
    key_grad = jnp.concatenate([grads[c, 0] for c in range(KVH)], axis=1)
    value_grad = jnp.concatenate([grads[c, 1] for c in range(KVH)], axis=1)
    return query_grad, key_grad, value_grad


def solution(mesh):
    row = jax.sharding.PartitionSpec(("grp", "blk"), None)
    flat = jax.sharding.PartitionSpec()
    return jax.shard_map(
        per_device,
        mesh=mesh,
        in_specs=(row, row, row, row, row, row, flat, flat),
        out_specs=(row, row, row),
        check_vma=False,
    )
```

time: 116 us -> 92.2 us (0.79)
  Pallas kernels: 105 us -> 84.9 us
  local copies, waits for them, and re-layouts: 6.3 us -> 4.04 us
  between operations: 1.97 us -> 0.67 us
    pallas_call x3 -> x1, Pallas kernels: 102 us -> 81.9 us  [per_device(): pl.pallas_call(functools.partial(fused_kernel, n, n_blk, m, 256), out_sha...]
    dynamic_slice x2 -> x0, local copies, waits for them, and re-layouts: 2.48 us -> none  [the longest x1 1.24 us: per_device(): lax.dynamic_slice_in_dim(key_block, me, 1)]
    unnamed x0 -> x3, local copies, waits for them, and re-layouts: none -> 1.5 us
    broadcast_in_dim x1 -> x0, local copies, waits for them, and re-layouts: 1.43 us -> none  [per_device(): lse = jnp.transpose(log_norm)[:, None, :]]
where the time goes in v2:
time: 92.2 us; the launch traced here: 92 us
  Pallas kernels  84.9 us (92%)
  local copies, waits for them, and re-layouts  4.04 us (4%)
  other arithmetic  2.44 us (3%)
    pallas_call x1, Pallas kernels, per_device(): pl.pallas_call(functools.partial(fused_kernel, n, n_blk, m, 256), out_sha...  81.9 us
    pallas_call x1, Pallas kernels, make_plan(): pl.pallas_call(functools.partial(plan_kernel, n), out_shape=jax.ShapeDtyp...  2.98 us

profile of v2, /device:TPU:15, one launch (start us, length us, event | category | flops | bytes accessed | tf_op | source)
XLA Modules:
  0.0 92.0 jit_solution(3204272702717699917)
XLA Ops:
  0.6 3.0 %shard_map.103.plan_ref = s32[161]{0:T(256)} custom-call(s32[32]{0:T(128)} %held_ref.1, s32[32]{0:T(128)} %key_ref.1), custom_call_target="tpu_custom_call" | custom-call | tf_op jit(solution)/shard_map/pallas_call | solution.py:68
  3.6 1.2 %slice_bitcast_fusion.6 = (bf16[1,640,128]{2,1,0:T(8,128)(2,1)S(1)}, bf16[1,640,128]{2,1,0:T(8,128)(2,1)S(1)}, bf16[1,640,128]{2,1,0:T(8,128)(2,1)S(1)}, bf16[1,640,128]{2,1,0:T(8,128)(2,1)S(1)}) fusion(bf16[640,256]{1,0:T(8,128)(2,1)} %param.10, bf16[640,256]{1,0:T(8,128)(2,1)} %param.9), kind=kLoop, calls=%fused_computation.9 | loop fusion | bytes 1310720 | tf_op jit(solution)/shard_map/stack | solution.py:325
  4.8 0.9 %pad_maximum_fusion = bf16[4,640,128]{2,1,0:T(8,128)(2,1)} fusion(bf16[1,640,128]{2,1,0:T(8,128)(2,1)S(1)} %get-tuple-element.14, bf16[1,640,128]{2,1,0:T(8,128)(2,1)S(1)} %get-tuple-element.15, bf16[1,640,128]{2,1,0:T(8,128)(2,1)S(1)} %get-tuple-element.13, bf16[1,640,128]{2,1,0:T(8,128)(2,1)S(1)} %get-tuple-element.16), kind=kLoop, calls=%fused_computation | loop fusion | flops 983040 | bytes 1310720 | tf_op jit(solution)/shard_map/stack | solution.py:325
  5.7 81.9 %shard_map.104 = (bf16[640,2048]{1,0:T(8,128)(2,1)}, bf16[32,80,128]{2,1,0:T(8,128)(2,1)}) custom-call(s32[161]{0:T(256)} %shard_map.103.plan_ref, bf16[32,80,128]{2,1,0:T(8,128)(2,1)} %bitcast.19, f32[16,640]{1,0:T(8,128)} %bitcast.21, bf16[640,2048]{1,0:T(8,128)(2,1)} %q_hbm.1, bf16[640,2048]{1,0:T(8,128)(2,1)} %do_hbm.1, bf16[640,2048]{1,0:T(8,128)(2,1)} %o_hbm.1), custom_call_target="tpu_custom_call" | custom-call | tf_op jit(solution)/shard_map/pallas_call | solution.py:334
  87.6 0.0 copy-start
  87.6 1.3 %slice_bitcast_fusion.1 = (bf16[640,128]{1,0:T(8,128)(2,1)S(1)}, bf16[640,128]{1,0:T(8,128)(2,1)S(1)}, bf16[640,128]{1,0:T(8,128)(2,1)S(1)}, bf16[640,128]{1,0:T(8,128)(2,1)S(1)}) fusion(bf16[2,2,640,128]{3,2,1,0:T(8,128)(2,1)} %bitcast.20), kind=kLoop, calls=%fused_computation.4 | loop fusion | bytes 1310720 | tf_op jit(solution)/shard_map/squeeze | solution.py:352
  89.0 0.8 pad_maximum_fusion.2
  89.8 0.8 pad_maximum_fusion.1
  90.5 0.0 copy-done
  90.5 1.5 %copy.12 = bf16[640,2048]{1,0:T(8,128)(2,1)} copy(bf16[640,2048]{1,0:T(8,128)(2,1)S(1)} %copy-done) | data formatting | bytes 5242880
Async XLA Ops:
  87.6 2.9 %copy-start = (bf16[640,2048]{1,0:T(8,128)(2,1)S(1)}, bf16[640,2048]{1,0:T(8,128)(2,1)}, u32[]{:S(2)}) copy-start(bf16[640,2048]{1,0:T(8,128)(2,1)} %get-tuple-element.20) | copy-start | bytes 7864324

commit v3 on v2

--- a/solution.py
+++ b/solution.py
@@ -19,61 +19,6 @@
     return [(at, min(width, rows - at)) for at in range(0, rows, width)]
 
 
-def plan_kernel(n, held_ref, key_ref, plan_ref, inv, count):
-    def zero(e, c):
-        count[e] = 0
-        return c
-
-    def invert(e, c):
-        inv[held_ref[e]] = e
-        return c
-
-    def hold(d, c):
-        e = inv[key_ref[d]]
-        plan_ref[d] = e
-        count[e] = count[e] + 1
-        return c
-
-    def prefix(e, at):
-        many = count[e]
-        count[e] = at
-        plan_ref[3 * n + e] = jnp.maximum(at + many - 1, 0)
-        plan_ref[4 * n + e] = jnp.minimum(many, 1)
-        return at + many
-
-    def place(d, c):
-        e = plan_ref[d]
-        at = count[e]
-        plan_ref[n + at] = d
-        plan_ref[2 * n + at] = inv[e]
-        inv[e] = 1
-        count[e] = at + 1
-        return c
-
-    def clear(e, c):
-        inv[e] = 0
-        return c
-
-    me = own_place()
-    plan_ref[5 * n] = jnp.where(held_ref[me] == key_ref[me], 1, 0)
-    lax.fori_loop(0, n, zero, 0)
-    lax.fori_loop(0, n, invert, 0)
-    lax.fori_loop(0, n, hold, 0)
-    lax.fori_loop(0, n, prefix, 0)
-    lax.fori_loop(0, n, clear, 0)
-    lax.fori_loop(0, n, place, 0)
-
-
-def make_plan(n, held_block, key_block):
-    return pl.pallas_call(
-        functools.partial(plan_kernel, n),
-        out_shape=jax.ShapeDtypeStruct((5 * n + 1,), jnp.int32),
-        in_specs=[pl.BlockSpec(memory_space=pltpu.SMEM)] * 2,
-        out_specs=pl.BlockSpec(memory_space=pltpu.SMEM),
-        scratch_shapes=[pltpu.SMEM((n,), jnp.int32), pltpu.SMEM((n,), jnp.int32)],
-    )(held_block, key_block)
-
-
 def own_place():
     return lax.axis_index("grp") * lax.axis_size("blk") + lax.axis_index("blk")
 
@@ -84,16 +29,19 @@
 
 
 def fused_kernel(
-    n, n_blk, m, width, plan_ref, kv_ref, lse_ref, q_hbm, do_hbm, o_hbm,
-    dq_hbm, out_ref,
+    n, n_blk, m, width, held_ref, key_ref, k_ref, v_ref, lse_ref, q_hbm, do_hbm, o_hbm,
+    dq_hbm, dk_ref, dv_ref,
     q_ref, do_ref, o_ref, dq_ref, lse3, delta3, held, picked, kv, pair, terms, sums, sent,
-    dk_acc, dv_acc, sems, local_sems,
+    dk_acc, dv_acc, holder, before, last_of, sems, local_sems,
 ):
     rows = q_ref.shape[0]
     half = m // 2
     me = own_place()
     kind = lax.rem(me, 2)
     slot = kind * half + me // 2
+    part = held.shape[1]
+    block_row = pl.multiple_of(lax.rem(me // 2, half // 2) * part, part)
+    of_keys = me // 2 < half // 2
     relay = me < m
     fetch_in, fetch_out, return_in, return_out = [sems.at[i] for i in range(4)]
     kv_out, kv_in, pair_out, grad_in = [(sems.at[i], sems.at[i + 1]) for i in range(4, 12, 2)]
@@ -137,18 +85,47 @@
         def _():
             dst[me] = src[slot]
 
+    def send_blocks(c):
+        cols = slice(c * DH, (c + 1) * DH)
+
+        def push(k, carry):
+            i = lax.rem(me // 2 + k, half // 2)
+            row = pl.multiple_of(i * part, part)
+            for src, at in ((k_ref, i), (v_ref, half // 2 + i)):
+                t = 2 * at + c
+
+                @pl.when(t != me)
+                def _():
+                    pltpu.make_async_remote_copy(
+                        src_ref=src.at[pl.ds(row, part), cols], dst_ref=held.at[me],
+                        send_sem=kv_out[c], recv_sem=fetch_in,
+                        device_id=place(t), device_id_type=MESH,
+                    ).start()
+
+            return carry
+
+        lax.fori_loop(0, half // 2, push, 0)
+        mine = jnp.logical_and(relay, kind == c)
+
+        @pl.when(jnp.logical_and(mine, of_keys))
+        def _():
+            held[me] = k_ref[pl.ds(block_row, part), cols]
+
+        @pl.when(jnp.logical_and(mine, jnp.logical_not(of_keys)))
+        def _():
+            held[me] = v_ref[pl.ds(block_row, part), cols]
+
     def from_relay(src, dst, send_sem, recv_sem):
         def push(k, carry):
             t = lax.rem(me + k, n)
             pltpu.make_async_remote_copy(
-                src_ref=src.at[t], dst_ref=dst.at[slot],
+                src_ref=src.at[t], dst_ref=dst,
                 send_sem=send_sem, recv_sem=recv_sem,
                 device_id=place(t), device_id_type=MESH,
             ).start()
             return carry
 
         lax.fori_loop(1, n, push, 0)
-        dst[slot] = src[me]
 
     def wait(ref, count, sem):
         part = ref.at[pl.ds(0, count)]
@@ -174,33 +151,43 @@
         wait(held, n - 1, fetch_in)
 
         def pick(d, carry):
-            picked[d] = held[plan_ref[d]]
+            picked[d] = held[holder[d]]
             return carry
 
         lax.fori_loop(0, n, pick, 0)
-        from_relay(picked, kv, fetch_out, kv_in[c])
+        from_relay(picked, kv.at[slot], fetch_out, kv_in[c])
+        kv[slot] = picked[me]
 
     def settle(c):
         wait(terms, n - 1, return_in)
 
-        def add(k, total):
-            term = terms[plan_ref[n + k]].astype(jnp.float32)
-            total = jnp.where(plan_ref[2 * n + k] == 1, total, 0.0) + term
-            sums[k] = total
-            return total
-
-        lax.fori_loop(0, n, add, jnp.zeros(sums.shape[1:], jnp.float32))
+        def add(d, carry):
+            earlier = before[d]
+            total = jnp.where(earlier >= 0, sums[jnp.maximum(earlier, 0)], 0.0)
+            sums[d] = total + terms[d].astype(jnp.float32)
+            return carry
+
+        sums[0] = jnp.zeros_like(sums[0])
+        lax.fori_loop(0, n, add, 0)
 
         def pick(e, carry):
-            total = sums[plan_ref[3 * n + e]]
-            sent[e] = jnp.where(plan_ref[4 * n + e] == 1, total, 0.0).astype(jnp.bfloat16)
+            d = last_of[e]
+            total = jnp.where(d >= 0, sums[jnp.maximum(d, 0)], 0.0)
+            sent[e] = total.astype(jnp.bfloat16)
             return carry
 
         lax.fori_loop(0, n, pick, 0)
-        from_relay(sent, out_ref, return_out, grad_in[c])
+        cols = slice(c * DH, (c + 1) * DH)
+        for dst, mine in ((dk_ref, of_keys), (dv_ref, jnp.logical_not(of_keys))):
+
+            @pl.when(mine)
+            def _():
+                spot = dst.at[pl.ds(block_row, part), cols]
+                from_relay(sent, spot, return_out, grad_in[c])
+                dst[pl.ds(block_row, part), cols] = sent[me]
 
     def heads(c, first, last):
-        diag = plan_ref[5 * n]
+        diag = jnp.where(held_ref[me] == key_ref[me], 1, 0)
         slack = rows * (1 - diag)
 
         def one(h, carry):
@@ -250,7 +237,27 @@
             dv_acc[...].astype(jnp.bfloat16).reshape(shape)
         )
 
-    to_relays(0, kv_ref, held, kv_out[0], fetch_in)
+    send_blocks(0)
+
+    def find(count, test, none):
+        def step(i, found):
+            return jnp.where(test(i), i, found)
+
+        return lax.fori_loop(0, count, step, none, unroll=8)
+
+    def plan_holder(d, carry):
+        block = key_ref[d]
+        holder[d] = find(n, lambda e: held_ref[e] == block, 0)
+        return carry
+
+    def plan_sums(d, carry):
+        own = holder[d]
+        before[d] = find(n, lambda i: jnp.logical_and(holder[i] == own, i < d), -1)
+        last_of[d] = find(n, lambda i: holder[i] == d, -1)
+        return carry
+
+    lax.fori_loop(0, n, plan_holder, 0)
+    lax.fori_loop(0, n, plan_sums, 0)
     for h in range(H):
         lse3[h] = lse_ref[h : h + 1, :] * LOG2E
     loads[0].wait()
@@ -269,13 +276,13 @@
     @pl.when(first)
     def _():
         deliver(0)
-        to_relays(1, kv_ref, held, kv_out[1], fetch_in)
+        send_blocks(1)
 
     wait_pieces(0, kv, kv_in[0])
 
     @pl.when(jnp.logical_not(first))
     def _():
-        to_relays(1, kv_ref, held, kv_out[1], fetch_in)
+        send_blocks(1)
 
     clear()
     heads(0, 0, GROUP // 2)
@@ -294,9 +301,9 @@
     save.start()
     on_relay(1, settle)
     for c in range(KVH):
-        wait_pieces(c, kv_ref, kv_out[c])
+        wait_pieces(c, kv, kv_out[c])
         wait_pieces(c, pair, pair_out[c])
-        wait_pieces(c, out_ref, grad_in[c])
+        wait_pieces(c, pair, grad_in[c])
 
     @pl.when(relay)
     def _():
@@ -320,9 +327,6 @@
     rows = queries.shape[0]
     m = relay_count(n, rows)
     part = 2 * KVH * rows // m
-    plan = make_plan(n, held_block, key_block)
-    cut = lambda x, c: x[:, c * DH : (c + 1) * DH]
-    kv_own = jnp.stack([cut(x, c) for c in range(KVH) for x in (key_rows, value_rows)])
     lse = jnp.transpose(log_norm)
     vmem = pl.BlockSpec(memory_space=pltpu.VMEM)
     hbm = pl.BlockSpec(memory_space=pl.ANY)
@@ -331,26 +335,26 @@
     by_device = pltpu.VMEM((n, part, DH), jnp.bfloat16)
     by_slot = pltpu.VMEM((m, part, DH), jnp.bfloat16)
     acc = pltpu.VMEM((rows, DH), jnp.float32)
-    query_grad, grads = pl.pallas_call(
+    small = pl.BlockSpec(memory_space=pltpu.SMEM)
+    narrow = jax.ShapeDtypeStruct(key_rows.shape, jnp.bfloat16)
+    return pl.pallas_call(
         functools.partial(fused_kernel, n, n_blk, m, 256),
         out_shape=(
             jax.ShapeDtypeStruct((rows, H * DH), jnp.bfloat16),
-            jax.ShapeDtypeStruct((m, part, DH), jnp.bfloat16),
+            narrow,
+            narrow,
         ),
-        in_specs=[pl.BlockSpec(memory_space=pltpu.SMEM), vmem, vmem, hbm, hbm, hbm],
-        out_specs=(hbm, vmem),
+        in_specs=[small, small, vmem, vmem, vmem, hbm, hbm, hbm],
+        out_specs=(hbm, vmem, vmem),
         scratch_shapes=[
             wide, wide, wide, wide, line, line,
             by_device, by_device, by_slot, by_slot, by_device,
             pltpu.VMEM((n, part, DH), jnp.float32), by_device,
-            acc, acc, pltpu.SemaphoreType.DMA((12,)), pltpu.SemaphoreType.DMA((3,)),
+            acc, acc, pltpu.SMEM((n,), jnp.int32), pltpu.SMEM((n,), jnp.int32),
+            pltpu.SMEM((n,), jnp.int32), pltpu.SemaphoreType.DMA((12,)), pltpu.SemaphoreType.DMA((3,)),
         ],
         compiler_params=pltpu.CompilerParams(collective_id=0, has_side_effects=True),
-    )(plan, kv_own.reshape(m, part, DH), lse, queries, out_grad, attn_out)
-    grads = grads.reshape(KVH, 2, rows, DH)
-    key_grad = jnp.concatenate([grads[c, 0] for c in range(KVH)], axis=1)
-    value_grad = jnp.concatenate([grads[c, 1] for c in range(KVH)], axis=1)
-    return query_grad, key_grad, value_grad
+    )(held_block, key_block, key_rows, value_rows, lse, queries, out_grad, attn_out)
 
 
 def solution(mesh):

time: 92.2 us -> 86.4 us (0.937)
  Pallas kernels: 84.9 us -> 80.5 us
  other arithmetic: 2.44 us -> 0 us
  local copies, waits for them, and re-layouts: 4.04 us -> 5.08 us
    unnamed x3 -> x7, local copies, waits for them, and re-layouts: 1.5 us -> 5.08 us
    pallas_call x1 -> x0, Pallas kernels: 2.98 us -> none  [make_plan(): pl.pallas_call(functools.partial(plan_kernel, n), out_shape=jax.ShapeDtyp...]
    concatenate x2 -> x0, other arithmetic: 1.52 us -> none  [the longest x1 0.76 us: per_device(): value_grad = jnp.concatenate([grads[c, 1] for c in range(KVH)], axis=1)]
    squeeze x1 -> x0, local copies, waits for them, and re-layouts: 1.35 us -> none  [per_device(): value_grad = jnp.concatenate([grads[c, 1] for c in range(KVH)], axis=1)]
    pallas_call x1, Pallas kernels: 81.9 us -> 80.5 us  [per_device(): pl.pallas_call(functools.partial(fused_kernel, n, n_blk, m, 256), out_sha...]
    another operation x1 -> x0, local copies, waits for them, and re-layouts: 1.2 us -> none  [per_device(): jnp.stack([cut(x, c) for c in range(KVH) for x in (key_rows, value_rows)])]
where the time goes in v3:
time: 86.4 us; the launch traced here: 86.3 us
  Pallas kernels  80.5 us (93%)
  local copies, waits for them, and re-layouts  5.08 us (6%)
    pallas_call x1, Pallas kernels, per_device(): pl.pallas_call(functools.partial(fused_kernel, n, n_blk, m, 256), out_sha...  80.5 us
    unnamed x7, local copies, waits for them, and re-layouts  5.08 us

profile of v3, /device:TPU:15, one launch (start us, length us, event | category | flops | bytes accessed | tf_op | source)
XLA Modules:
  0.0 86.3 jit_solution(6285016992215346174)
XLA Ops:
  0.6 80.5 %shard_map.103 = (bf16[640,2048]{1,0:T(8,128)(2,1)}, bf16[640,256]{1,0:T(8,128)(2,1)}, bf16[640,256]{1,0:T(8,128)(2,1)}) custom-call(s32[32]{0:T(128)} %held_ref.1, s32[32]{0:T(128)} %key_ref.1, bf16[640,256]{1,0:T(8,128)(2,1)} %k_ref.1, bf16[640,256]{1,0:T(8,128)(2,1)} %v_ref.1, f32[16,640]{1,0:T(8,128)} %bitcast.1, bf16[640,2048]{1,0:T(8,128)(2,1)} %q_hbm.1, ...), custom_call_target="tpu_custom_call" | custom-call | tf_op jit(solution)/shard_map/pallas_call | solution.py:340
  81.2 0.0 copy-start.1
  81.2 0.0 copy-start
  81.2 3.6 %copy.14 = bf16[640,2048]{1,0:T(8,128)(2,1)} copy(bf16[640,2048]{1,0:T(8,128)(2,1)} %get-tuple-element.6) | data formatting | bytes 5242880
  84.8 0.0 copy-done.1
  84.8 0.7 copy.15
  85.6 0.0 copy-done
  85.6 0.7 copy.16
Async XLA Ops:
  81.2 3.6 %copy-start.1 = (bf16[640,256]{1,0:T(8,128)(2,1)S(1)}, bf16[640,256]{1,0:T(8,128)(2,1)}, u32[]{:S(2)}) copy-start(bf16[640,256]{1,0:T(8,128)(2,1)} %get-tuple-element.7) | copy-start | bytes 983044
  81.2 4.4 %copy-start = (bf16[640,256]{1,0:T(8,128)(2,1)S(1)}, bf16[640,256]{1,0:T(8,128)(2,1)}, u32[]{:S(2)}) copy-start(bf16[640,256]{1,0:T(8,128)(2,1)} %get-tuple-element.8) | copy-start | bytes 983044

commit v4 on v3

--- a/solution.py
+++ b/solution.py
@@ -202,15 +202,20 @@
                 delta = delta3[h, :, at : at + w]
                 s = lax.dot_general(k, q, NT, preferred_element_type=jnp.float32)
                 s = s * (SCALE * LOG2E)
+                i = lax.broadcasted_iota(jnp.int32, lse.shape, 1) + (at + slack)
                 parts = []
-                if at:
-                    parts.append(jnp.exp2(s[:at] - lse))
-                square = jnp.exp2(s[at : at + w] - lse)
-                j = lax.broadcasted_iota(jnp.int32, square.shape, 0)
-                i = lax.broadcasted_iota(jnp.int32, square.shape, 1)
-                parts.append(jnp.where(j - i <= slack, square, 0.0))
-                if at + w < rows:
-                    parts.append(jnp.exp2(s[at + w :] - jnp.where(diag == 1, FAR, lse)))
+                for low, size in chunks_of(rows, DH):
+                    line = jnp.where(i < low, FAR, lse)
+                    block = jnp.exp2(s[low : low + size] - line)
+                    if at <= low < at + w:
+                        left = low - at
+                        square = block[:, left : left + size]
+                        below = lax.broadcasted_iota(jnp.int32, square.shape, 0)
+                        right = lax.broadcasted_iota(jnp.int32, square.shape, 1)
+                        square = jnp.where(below - right <= slack, square, 0.0)
+                        pieces = [block[:, :left], square, block[:, left + size :]]
+                        block = jnp.concatenate([x for x in pieces if x.shape[1]], axis=1)
+                    parts.append(block)
                 p = jnp.concatenate(parts, axis=0)
                 dp = lax.dot_general(v, do, NT, preferred_element_type=jnp.float32)
                 ds = (p * (dp - delta)).astype(jnp.bfloat16)
@@ -338,7 +343,7 @@
     small = pl.BlockSpec(memory_space=pltpu.SMEM)
     narrow = jax.ShapeDtypeStruct(key_rows.shape, jnp.bfloat16)
     return pl.pallas_call(
-        functools.partial(fused_kernel, n, n_blk, m, 256),
+        functools.partial(fused_kernel, n, n_blk, m, rows),
         out_shape=(
             jax.ShapeDtypeStruct((rows, H * DH), jnp.bfloat16),
             narrow,

time: 86.4 us -> 86 us (level)
  no operation moved by 1% of the time
where the time goes in v4:
time: 86 us; the launch traced here: 85.8 us
  Pallas kernels  80.1 us (93%)
  local copies, waits for them, and re-layouts  5.08 us (6%)
    pallas_call x1, Pallas kernels, per_device(): pl.pallas_call(functools.partial(fused_kernel, n, n_blk, m, rows), out_sh...  80.1 us
    unnamed x7, local copies, waits for them, and re-layouts  5.08 us

profile of v4, /device:TPU:15, one launch (start us, length us, event | category | flops | bytes accessed | tf_op | source)
XLA Modules:
  0.0 85.8 jit_solution(12010454441947727958)
XLA Ops:
  0.6 80.1 %shard_map.103 = (bf16[640,2048]{1,0:T(8,128)(2,1)}, bf16[640,256]{1,0:T(8,128)(2,1)}, bf16[640,256]{1,0:T(8,128)(2,1)}) custom-call(s32[32]{0:T(128)} %held_ref.1, s32[32]{0:T(128)} %key_ref.1, bf16[640,256]{1,0:T(8,128)(2,1)} %k_ref.1, bf16[640,256]{1,0:T(8,128)(2,1)} %v_ref.1, f32[16,640]{1,0:T(8,128)} %bitcast.1, bf16[640,2048]{1,0:T(8,128)(2,1)} %q_hbm.1, ...), custom_call_target="tpu_custom_call" | custom-call | tf_op jit(solution)/shard_map/pallas_call | solution.py:345
  80.8 0.0 copy-start.1
  80.8 0.0 copy-start
  80.8 3.6 %copy.14 = bf16[640,2048]{1,0:T(8,128)(2,1)} copy(bf16[640,2048]{1,0:T(8,128)(2,1)} %get-tuple-element.6) | data formatting | bytes 5242880
  84.4 0.0 copy-done.1
  84.4 0.7 copy.15
  85.1 0.0 copy-done
  85.1 0.7 copy.16
Async XLA Ops:
  80.8 3.6 %copy-start.1 = (bf16[640,256]{1,0:T(8,128)(2,1)S(1)}, bf16[640,256]{1,0:T(8,128)(2,1)}, u32[]{:S(2)}) copy-start(bf16[640,256]{1,0:T(8,128)(2,1)} %get-tuple-element.7) | copy-start | bytes 983044
  80.8 4.4 %copy-start = (bf16[640,256]{1,0:T(8,128)(2,1)S(1)}, bf16[640,256]{1,0:T(8,128)(2,1)}, u32[]{:S(2)}) copy-start(bf16[640,256]{1,0:T(8,128)(2,1)} %get-tuple-element.8) | copy-start | bytes 983044

commit v5 on v4

--- a/solution.py
+++ b/solution.py
@@ -283,12 +283,11 @@
         deliver(0)
         send_blocks(1)
 
-    wait_pieces(0, kv, kv_in[0])
-
     @pl.when(jnp.logical_not(first))
     def _():
         send_blocks(1)
 
+    wait_pieces(0, kv, kv_in[0])
     clear()
     heads(0, 0, GROUP // 2)
     on_relay(1, deliver)

time: 86 us -> 82.2 us (0.956)
  Pallas kernels: 80.1 us -> 75.9 us
    pallas_call x1, Pallas kernels: 80.1 us -> 75.9 us  [per_device(): pl.pallas_call(functools.partial(fused_kernel, n, n_blk, m, rows), out_sh...]
where the time goes in v5:
time: 82.2 us; the launch traced here: 81.6 us
  Pallas kernels  75.9 us (92%)
  local copies, waits for them, and re-layouts  5.08 us (6%)
    pallas_call x1, Pallas kernels, per_device(): pl.pallas_call(functools.partial(fused_kernel, n, n_blk, m, rows), out_sh...  75.9 us
    unnamed x7, local copies, waits for them, and re-layouts  5.08 us

profile of v5, /device:TPU:15, one launch (start us, length us, event | category | flops | bytes accessed | tf_op | source)
XLA Modules:
  0.0 81.6 jit_solution(8021676519827774347)
XLA Ops:
  0.6 75.9 %shard_map.103 = (bf16[640,2048]{1,0:T(8,128)(2,1)}, bf16[640,256]{1,0:T(8,128)(2,1)}, bf16[640,256]{1,0:T(8,128)(2,1)}) custom-call(s32[32]{0:T(128)} %held_ref.1, s32[32]{0:T(128)} %key_ref.1, bf16[640,256]{1,0:T(8,128)(2,1)} %k_ref.1, bf16[640,256]{1,0:T(8,128)(2,1)} %v_ref.1, f32[16,640]{1,0:T(8,128)} %bitcast.1, bf16[640,2048]{1,0:T(8,128)(2,1)} %q_hbm.1, ...), custom_call_target="tpu_custom_call" | custom-call | tf_op jit(solution)/shard_map/pallas_call | solution.py:344
  76.5 0.0 copy-start.1
  76.5 0.0 copy-start
  76.5 3.6 %copy.14 = bf16[640,2048]{1,0:T(8,128)(2,1)} copy(bf16[640,2048]{1,0:T(8,128)(2,1)} %get-tuple-element.6) | data formatting | bytes 5242880
  80.1 0.0 copy-done.1
  80.1 0.7 copy.15
  80.9 0.0 copy-done
  80.9 0.7 copy.16
Async XLA Ops:
  76.5 3.6 %copy-start.1 = (bf16[640,256]{1,0:T(8,128)(2,1)S(1)}, bf16[640,256]{1,0:T(8,128)(2,1)}, u32[]{:S(2)}) copy-start(bf16[640,256]{1,0:T(8,128)(2,1)} %get-tuple-element.7) | copy-start | bytes 983044
  76.5 4.4 %copy-start = (bf16[640,256]{1,0:T(8,128)(2,1)S(1)}, bf16[640,256]{1,0:T(8,128)(2,1)}, u32[]{:S(2)}) copy-start(bf16[640,256]{1,0:T(8,128)(2,1)} %get-tuple-element.8) | copy-start | bytes 983044
